TPU v7x, 32 devices: a whole 2x2x4 slice. The times are simulated.
32 devices in a mesh: groups: 2 (over y), aux: 4 (over z), pts: 2 (over x), rep: 2 (over core).
Axes of the slice: x: 2, y: 2, z: 4, core: 2. Of those that a mesh axis runs over, the one named last changes fastest.
Arguments:
- density_slab: bfloat16 [32, 1024, 1024], P('groups', 'aux', 'rep'), parts along dimension 0, may hold values from -0.005859375 to 0.005859375
- orbitals: bfloat16 [2048, 8192], P(('groups', 'rep'), 'pts'), parts along dimension 0, may hold values from -6 to 6
Outputs:
- rhs_share: float32 [16384, 8192], P(('groups', 'pts'), ('aux', 'rep')), parts along dimension 0
There are 2 independent parts, one for each index of `groups`. A program takes and returns all parts, laid end to end along the dimension named above; each array names one. Nothing has to cross between parts.
All inputs are finite; a program needn't handle non-finite values.
Results may differ from a plain program's by a relative error of at most 0.0003.
Values may be sent and summed in bfloat16 or wider, within the bound.
A program may use at most 64 MiB of HBM per device.

v0:
```python
import jax
import jax.numpy as jnp
from jax import lax
from jax.sharding import PartitionSpec as P


def spread_points(own_weights):
    return lax.all_gather(own_weights, "pts", axis=1, tiled=True)


def all_rows(orbitals):
    return lax.all_gather(orbitals, "rep", axis=0, tiled=True)


def per_device(density_slab, orbitals):
    aux_index = lax.axis_index("aux")
    rep_index = lax.axis_index("rep")
    n_aux = lax.axis_size("aux")
    n_rep = lax.axis_size("rep")
    full_orbitals = all_rows(orbitals)
    regrouped = lax.all_to_all(density_slab, "aux", split_axis=0, concat_axis=1, tiled=True)
    contracted = jnp.einsum("kpq,qs->kps", regrouped, orbitals, preferred_element_type=jnp.float32)
    partial_w = jnp.sum(full_orbitals[None] * contracted, axis=1)
    summed = lax.psum(partial_w, "rep")
    own_w = lax.all_gather(summed, "aux", axis=0, tiled=True)
    all_w = spread_points(own_w)
    col_width = all_w.shape[1] // (n_aux * n_rep)
    column_w = lax.dynamic_slice_in_dim(
        all_w, (aux_index * n_rep + rep_index) * col_width, col_width, 1
    )
    share = jnp.dot(
        own_w.T, column_w, precision=lax.Precision.HIGHEST, preferred_element_type=jnp.float32
    )
    return share / jnp.float32(own_w.shape[0])


def solution(mesh):
    return jax.shard_map(
        per_device,
        mesh=mesh,
        in_specs=(P("groups", "aux", "rep"), P(("groups", "rep"), "pts")),
        out_specs=P(("groups", "pts"), ("aux", "rep")),
        check_vma=False,
    )
```

profile of v0, /device:TPU:0, one launch (start us, length us, event | category | flops | bytes accessed | tf_op | source)
XLA Modules:
  0.0 205.3 jit_solution(8422975068167474057)
XLA Ops:
  6.5 0.0 all-gather.3.cloned.1.call-start
  6.5 0.7 all-gather.3.cloned.1.call-update
  7.3 0.0 all-reduce.2.cloned.1.call-start
  7.3 99.5 %all_to_all.18 = bf16[16,256,512]{2,1,0:T(8,128)(2,1)S(1)} all-to-all(bf16[16,256,512]{2,1,0:T(8,128)(2,1)} %param.2), channel_id=1, replica_groups=mesh['groups'=2,'aux'=4,'pts'=2,'rep'=2] {'aux'}, dimensions={0} | all-to-all | bytes 8388608 | tf_op jit(solution)/shard_map/all_to_all | solution.py:21
  106.8 2.4 %copy.4 = bf16[4,4,256,512]{3,2,0,1:T(8,128)(2,1)} copy(bf16[4,4,256,512]{3,2,1,0:T(8,128)(2,1)S(1)} %bitcast.10) | data formatting | bytes 8388608 | tf_op jit(solution)/shard_map/all_to_all | solution.py:21
  109.2 0.0 all-gather.3.cloned.1.call-done
  109.2 0.0 copy-start
  109.2 12.0 %convert_element_type.4 = f32[1024,4096]{1,0:T(8,128)} convert(bf16[1024,4096]{1,0:T(8,128)(2,1)} %all-gather.3.cloned.1.call-done) | non-fusion elementwise | flops 4194304 | bytes 25165824 | tf_op jit(solution)/shard_map/convert_element_type | solution.py:23
  121.1 0.0 copy-done
  121.1 22.4 %multiply_reduce_fusion = f32[4,4096]{1,0:T(4,128)} fusion(bf16[4,1024,512]{2,1,0:T(8,128)(2,1)} %bitcast.11, f32[1024,4096]{1,0:T(8,128)} %convert_element_type.4, bf16[512,4096]{1,0:T(8,128)(2,1)S(1)} %copy-done), kind=kOutput, calls=%fused_computation | convolution fusion | flops 17213407232 | bytes 25231360 | tf_op jit(solution)/shard_map/kpq,qs->kps/dot_general | solution.py:22
  143.5 0.0 all-reduce.2.cloned.1.call-update
  143.6 17.2 %all-reduce.2.cloned.1.call-done = f32[4,4096]{1,0:T(4,128)} async-done(((f32[4,4096]{1,0:T(4,128)}), f32[4,4096]{1,0:T(4,128)}) %all-reduce.2.cloned.1.call-update) | async-done | bytes 65552 | tf_op jit(solution)/shard_map/psum | solution.py:24
  160.8 14.4 %all-gather = f32[4,4,4096]{2,1,0:T(4,128)S(1)} all-gather(f32[1,4,4096]{2,1,0:T(4,128)} %bitcast.12), channel_id=1, replica_groups=mesh['groups'=2,'aux'=4,'pts'=2,'rep'=2] {'aux'}, dimensions={0}, use_global_device_ids=true | all-gather | bytes 327680 | tf_op jit(solution)/shard_map/all_gather | solution.py:25
  175.2 0.1 reshape.3
  175.3 7.2 %all_gather.11 = f32[16,8192]{1,0:T(8,128)S(1)} all-gather(f32[16,4096]{1,0:T(8,128)S(1)} %reshape.3), channel_id=1, replica_groups=mesh['groups'=2,'aux'=4,'pts'=2,'rep'=2] {'pts'}, dimensions={1}, use_global_device_ids=true | all-gather | bytes 786432 | tf_op jit(solution)/shard_map/all_gather | solution.py:8
  182.6 15.9 %convolution_multiply_fusion = f32[4096,1024]{1,0:T(8,128)} fusion(f32[16,4096]{1,0:T(8,128)S(1)} %reshape.3, f32[16,8192]{1,0:T(8,128)S(1)} %all_gather.11, s32[]{:T(128)S(6)} %select_n.3), kind=kOutput, calls=%fused_computation.1 | convolution fusion | flops 809500672 | bytes 17104900 | tf_op jit(solution)/shard_map/dot_general | solution.py:31
Async XLA Ops:
  6.5 102.6 %all-gather.3.cloned.1.call-start = ((), (), s32[]{:S(2)}) async-start(), calls=%async_computation.1 | async-start | bytes 12582912 | tf_op jit(solution)/shard_map/all_gather | solution.py:12
  7.3 153.5 %all-reduce.2.cloned.1.call-start = ((), (), s32[]{:S(2)}) async-start(), calls=%async_computation.2 | async-start | bytes 131072 | tf_op jit(solution)/shard_map/psum | solution.py:24
  109.2 12.0 %copy-start = (bf16[512,4096]{1,0:T(8,128)(2,1)S(1)}, bf16[512,4096]{1,0:T(8,128)(2,1)}, u32[]{:S(2)}) copy-start(bf16[512,4096]{1,0:T(8,128)(2,1)} %param.3) | copy-start | bytes 12582916
Sparse Core Ops, SparseCore 0:
  8.9 22.5 all-gather.2
  143.7 17.0 all-reduce.1
where the time goes:
time: 206 us; the launch traced here: 205 us
  blocking collectives  121 us (59%)
  matrix products  38.3 us (19%)
  waiting for transfers between devices  18 us (9%)
  between operations  13.4 us (7%)
  other arithmetic  12 us (6%)
  local copies, waits for them, and re-layouts  2.48 us (1%)
    all_to_all x1, blocking collectives, per_device(): lax.all_to_all(density_slab, 'aux', split_axis=0, concat_axis=1, tiled=True)  99.5 us
    dot_general x1, matrix products, per_device(): jnp.einsum('kpq,qs->kps', regrouped, orbitals, preferred_element_type=jnp...  22.4 us
    psum x1, waiting for transfers between devices, per_device(): summed = lax.psum(partial_w, 'rep')  17.2 us
    dot_general x1, matrix products, per_device(): jnp.dot(own_w.T, column_w, precision=lax.Precision.HIGHEST, preferred_ele...  15.9 us
    all_gather x1, blocking collectives, per_device(): own_w = lax.all_gather(summed, 'aux', axis=0, tiled=True)  14.4 us
    convert_element_type x1, other arithmetic, per_device(): partial_w = jnp.sum(full_orbitals[None] * contracted, axis=1)  12 us
    all_gather x1, blocking collectives, spread_points(): return lax.all_gather(own_weights, 'pts', axis=1, tiled=True)  7.24 us
  transfers between devices with their start and end apart: 2, of which 1 were waited for; matrix products, arithmetic and copies ran while one was open for 1% of the time, Pallas kernels for 0%

commit v1 on v0

v1 whole, which is shorter than its diff:
```python
import functools

import jax
import jax.numpy as jnp
from jax import lax
from jax.experimental import pallas as pl
from jax.experimental.pallas import tpu as pltpu
from jax.sharding import PartitionSpec as P


def weights_kernel(group, d_ref, q_ref, p_ref, w_ref):
    n_k, n_p, n_q = d_ref.shape
    q_rows = q_ref[...]
    p_rows = p_ref[...].astype(jnp.float32)
    for k in range(0, n_k, group):
        lhs = d_ref[k : k + group].reshape(group * n_p, n_q)
        c = jnp.dot(lhs, q_rows, preferred_element_type=jnp.float32)
        for j in range(group):
            part = c[j * n_p : (j + 1) * n_p] * p_rows
            w_ref[k + j : k + j + 1, :] = jnp.sum(part, axis=0, keepdims=True)


def partial_weights(density, q_rows, p_rows, tile=512, group=4):
    n_k, n_p, n_q = density.shape
    n_pts = q_rows.shape[1]
    tile = min(tile, n_pts)
    return pl.pallas_call(
        functools.partial(weights_kernel, group),
        grid=(n_pts // tile,),
        in_specs=[
            pl.BlockSpec((n_k, n_p, n_q), lambda i: (0, 0, 0), pipeline_mode=pl.Buffered(1)),
            pl.BlockSpec((n_q, tile), lambda i: (0, i)),
            pl.BlockSpec((n_p, tile), lambda i: (0, i)),
        ],
        out_specs=pl.BlockSpec((n_k, tile), lambda i: (0, i)),
        out_shape=jax.ShapeDtypeStruct((n_k, n_pts), jnp.float32),
        compiler_params=pltpu.CompilerParams(vmem_limit_bytes=48 << 20),
        cost_estimate=pl.CostEstimate(
            flops=2 * n_k * n_p * n_q * n_pts,
            bytes_accessed=2 * (n_k * n_p * n_q + (n_p + n_q) * n_pts),
            transcendentals=0,
        ),
    )(density, q_rows, p_rows)


def split(w):
    high = w.astype(jnp.bfloat16)
    return high, (w - high.astype(jnp.float32)).astype(jnp.bfloat16)


def outer_kernel(scale, row_ref, col_ref, o_ref):
    r_hi, r_lo = split(row_ref[...])
    c_hi, c_lo = split(col_ref[...])
    left = jnp.concatenate([r_hi, r_hi, r_lo], axis=0)
    right = jnp.concatenate([c_hi, c_lo, c_hi], axis=0)
    o_ref[...] = (
        lax.dot_general(
            left, right, (((0,), (0,)), ((), ())), preferred_element_type=jnp.float32
        )
        * scale
    )


def outer(row_w, col_w, tile=512):
    n_k, n_rows = row_w.shape
    n_cols = col_w.shape[1]
    tile = min(tile, n_rows)
    return pl.pallas_call(
        functools.partial(outer_kernel, 1.0 / n_k),
        grid=(n_rows // tile,),
        in_specs=[
            pl.BlockSpec((n_k, tile), lambda i: (0, i)),
            pl.BlockSpec((n_k, n_cols), lambda i: (0, 0)),
        ],
        out_specs=pl.BlockSpec((tile, n_cols), lambda i: (i, 0)),
        out_shape=jax.ShapeDtypeStruct((n_rows, n_cols), jnp.float32),
        compiler_params=pltpu.CompilerParams(vmem_limit_bytes=32 << 20),
    )(row_w, col_w)


def per_device(density_slab, orbitals):
    aux_index = lax.axis_index("aux")
    rep_index = lax.axis_index("rep")
    n_aux = lax.axis_size("aux")
    n_rep = lax.axis_size("rep")
    n_p = density_slab.shape[1]
    first = aux_index * n_p
    owner = first // orbitals.shape[0]
    ship = lax.dynamic_slice_in_dim(orbitals, first % orbitals.shape[0], n_p, 0)
    both = lax.all_gather(ship, "rep", axis=0)
    p_rows = lax.dynamic_index_in_dim(both, owner, 0, keepdims=False)
    own_w = lax.psum(partial_weights(density_slab, orbitals, p_rows), ("aux", "rep"))
    all_w = lax.all_gather(own_w, "pts", axis=1, tiled=True)
    col_width = all_w.shape[1] // (n_aux * n_rep)
    column_w = lax.dynamic_slice_in_dim(
        all_w, (aux_index * n_rep + rep_index) * col_width, col_width, 1
    )
    return outer(own_w, column_w)


def solution(mesh):
    return jax.shard_map(
        per_device,
        mesh=mesh,
        in_specs=(P("groups", "aux", "rep"), P(("groups", "rep"), "pts")),
        out_specs=P(("groups", "pts"), ("aux", "rep")),
        check_vma=False,
    )
```

time: 206 us -> 129 us (0.63)
  blocking collectives: 121 us -> 7.25 us
  waiting for transfers between devices: 18 us -> 72.8 us
  matrix products: 38.3 us -> 0 us
  Pallas kernels: 0 us -> 29.8 us
  other arithmetic: 12 us -> 0 us
  local copies, waits for them, and re-layouts: 2.48 us -> 5.88 us
    all_to_all x1 -> x0, blocking collectives: 99.5 us -> none  [per_device(): lax.all_to_all(density_slab, 'aux', split_axis=0, concat_axis=1, tiled=True)]
    psum x1, waiting for transfers between devices: 17.2 us -> 56.3 us  [per_device(): lax.psum(partial_weights(density_slab, orbitals, p_rows), ('aux', 'rep'))]
    dot_general x2 -> x0, matrix products: 38.3 us -> none  [the longest x1 22.4 us: per_device(): jnp.einsum('kpq,qs->kps', regrouped, orbitals, preferred_element_type=jnp...]
    pallas_call x0 -> x2, Pallas kernels: none -> 29.8 us  [the longest x1 22 us: partial_weights(): pl.pallas_call(functools.partial(weights_kernel, group), grid=(n_pts // t...]
    all_gather x1, waiting for transfers between devices: 0.01 us -> 16.5 us  [per_device(): both = lax.all_gather(ship, 'rep', axis=0)]
    all_gather x2 -> x1, blocking collectives: 21.7 us -> 7.25 us  [per_device(): all_w = lax.all_gather(own_w, 'pts', axis=1, tiled=True)]
    convert_element_type x1 -> x0, other arithmetic: 12 us -> none  [per_device(): partial_w = jnp.sum(full_orbitals[None] * contracted, axis=1)]
    dynamic_slice x0 -> x2, local copies, waits for them, and re-layouts: none -> 3.13 us  [the longest x1 3.13 us: per_device(): ship = lax.dynamic_slice_in_dim(orbitals, first % orbitals.shape[0], n_p, 0)]
  transfers between devices with their start and end apart: 2 -> 2, of which waited for: 1 -> 2; matrix products, arithmetic and copies ran while one was open for 1% -> 0% of each run, Pallas kernels for 0% -> 0%
where the time goes in v1:
time: 129 us
  waiting for transfers between devices  72.8 us (56%)
  Pallas kernels  29.8 us (23%)
  between operations  13.4 us (10%)
  blocking collectives  7.25 us (6%)
  local copies, waits for them, and re-layouts  5.88 us (5%)
    psum x1, waiting for transfers between devices, per_device(): lax.psum(partial_weights(density_slab, orbitals, p_rows), ('aux', 'rep'))  56.3 us
    pallas_call x1, Pallas kernels, partial_weights(): pl.pallas_call(functools.partial(weights_kernel, group), grid=(n_pts // t...  22 us
    all_gather x1, waiting for transfers between devices, per_device(): both = lax.all_gather(ship, 'rep', axis=0)  16.5 us
    pallas_call x1, Pallas kernels, outer(): pl.pallas_call(functools.partial(outer_kernel, 1.0 / n_k), grid=(n_rows /...  7.8 us
    all_gather x1, blocking collectives, per_device(): all_w = lax.all_gather(own_w, 'pts', axis=1, tiled=True)  7.25 us
    dynamic_slice x1, local copies, waits for them, and re-layouts, per_device(): ship = lax.dynamic_slice_in_dim(orbitals, first % orbitals.shape[0], n_p, 0)  3.13 us
  transfers between devices with their start and end apart: 2, of which 2 were waited for; matrix products, arithmetic and copies ran while one was open for 0% of the time, Pallas kernels for 0%

profile of v1, /device:TPU:0, one launch (start us, length us, event | category | flops | bytes accessed | tf_op | source)
XLA Modules:
  0.0 129.2 jit_solution(9205936483264083971)
XLA Ops:
  6.5 0.0 all-gather.3.cloned.1.call-start
  6.5 3.1 %constant_dynamic-slice_fusion.1 = bf16[256,4096]{1,0:T(8,128)(2,1)} fusion(bf16[512,4096]{1,0:T(8,128)(2,1)} %q_ref.1, s32[]{:T(128)S(6)} %select_n.22), kind=kLoop, calls=%fused_computation.2 | loop fusion | bytes 4194308 | tf_op jit(solution)/shard_map/dynamic_slice | solution.py:89
  9.7 0.0 all-gather.3.cloned.1.call-update
  9.7 0.0 all-reduce.2.cloned.1.call-start
  9.8 16.5 %all-gather.3.cloned.1.call-done = bf16[512,4096]{1,0:T(8,128)(2,1)} async-done(((bf16[256,4096]{1,0:T(8,128)(2,1)}), bf16[512,4096]{1,0:T(8,128)(2,1)}) %all-gather.3.cloned.1.call-update) | async-done | bytes 4194320 | tf_op jit(solution)/shard_map/all_gather | solution.py:90
  26.2 1.8 %dynamic-slice_bitcast_fusion.p_ref = bf16[256,4096]{1,0:T(8,128)(2,1)S(1)} fusion(bf16[2,256,4096]{2,1,0:T(8,128)(2,1)} %bitcast.3, s32[]{:T(128)S(6)} %select_n.24), kind=kLoop, calls=%fused_computation | loop fusion | bytes 4194308 | tf_op jit(solution)/shard_map/jit(dynamic_index_in_dim)/squeeze | solution.py:91
  28.0 22.0 %shard_map.28 = f32[16,4096]{1,0:T(8,128)} custom-call(bf16[16,256,512]{2,1,0:T(8,128)(2,1)} %d_ref.1, bf16[512,4096]{1,0:T(8,128)(2,1)} %q_ref.1, bf16[256,4096]{1,0:T(8,128)(2,1)S(1)} %dynamic-slice_bitcast_fusion.p_ref), custom_call_target="tpu_custom_call" | custom-call | flops 17179869184 | bytes 10485760 | tf_op jit(solution)/shard_map/pallas_call | solution.py:27
  50.0 0.0 all-reduce.2.cloned.1.call-update
  50.1 56.3 %all-reduce.2.cloned.1.call-done.row_ref = f32[16,4096]{1,0:T(8,128)} async-done(((f32[16,4096]{1,0:T(8,128)}), f32[16,4096]{1,0:T(8,128)}) %all-reduce.2.cloned.1.call-update) | async-done | bytes 262160 | tf_op jit(solution)/shard_map/psum | solution.py:92
  106.4 7.2 %all_gather.11 = f32[16,8192]{1,0:T(8,128)S(1)} all-gather(f32[16,4096]{1,0:T(8,128)} %all-reduce.2.cloned.1.call-done.row_ref), channel_id=1, replica_groups=mesh['groups'=2,'aux'=4,'pts'=2,'rep'=2] {'pts'}, dimensions={1}, use_global_device_ids=true | all-gather | bytes 786432 | tf_op jit(solution)/shard_map/all_gather | solution.py:93
  113.6 0.0 copy-start
  113.6 0.9 copy-done
  114.6 7.8 %shard_map.29 = f32[4096,1024]{1,0:T(8,128)} custom-call(f32[16,4096]{1,0:T(8,128)S(1)} %copy-done, f32[16,1024]{1,0:T(8,128)S(1)} %constant_dynamic-slice_fusion.col_ref), custom_call_target="tpu_custom_call" | custom-call | tf_op jit(solution)/shard_map/pallas_call | solution.py:68
  (1 shorter events, 0.0 us)
Async XLA Ops:
  6.5 19.7 %all-gather.3.cloned.1.call-start = ((), (), s32[]{:S(2)}) async-start(), calls=%async_computation.1 | async-start | bytes 6291456 | tf_op jit(solution)/shard_map/all_gather | solution.py:90
  9.7 96.7 %all-reduce.2.cloned.1.call-start = ((), (), s32[]{:S(2)}) async-start(), calls=%async_computation | async-start | bytes 524288 | tf_op jit(solution)/shard_map/psum | solution.py:92
  113.6 1.0 copy-start
Sparse Core Ops, SparseCore 0:
  9.8 16.3 all-gather.2
  50.2 56.1 all-reduce.1

commit v2 on v0

v2 whole, which is shorter than its diff:
```python
import functools

import jax
import jax.numpy as jnp
from jax import lax
from jax.experimental import pallas as pl
from jax.experimental.pallas import tpu as pltpu
from jax.sharding import PartitionSpec as P


MESH = pl.DeviceIdType.MESH


def split(w):
    high = w.astype(jnp.bfloat16)
    return high, (w - high.astype(jnp.float32)).astype(jnp.bfloat16)


def share_kernel(
    sizes, d_hbm, orb_hbm, left_ref, right_ref,
    d_buf, q_buf, p_buf, part, rs_buf, ag_buf, col_buf, flat, col_flat,
    d_sem, q_sem, p_sem, ps_sem, rs_send, rs_recv, ag_send, ag_recv, col_send, col_recv,
):
    n_aux, n_pts, n_rep, group, tile = sizes
    n_k, n_p, n_q = d_hbm.shape
    members = n_aux * n_rep
    chunks, _, rows, width = part.shape
    a, x, r = lax.axis_index("aux"), lax.axis_index("pts"), lax.axis_index("rep")
    me = a * n_rep + r
    home = me // chunks
    first = a * n_p
    owner, offset = first // n_q, pl.multiple_of(first % n_q, n_p)

    def member(j):
        return {"aux": j // n_rep, "rep": j % n_rep}

    def cols(g):
        return pl.ds(pl.multiple_of(g * width, width), width)

    def d_copy(i):
        ks = pl.ds(i * group, group)
        return pltpu.make_async_copy(d_hbm.at[ks], d_buf.at[ks], d_sem.at[i])

    def q_copy(g):
        return pltpu.make_async_copy(orb_hbm.at[:, cols(g)], q_buf.at[g], q_sem.at[g])

    def p_local(g):
        return pltpu.make_async_copy(
            orb_hbm.at[pl.ds(offset, n_p), cols(g)], p_buf.at[g], p_sem.at[g]
        )

    def p_remote(g, step):
        return pltpu.make_async_remote_copy(
            orb_hbm.at[pl.ds(offset, n_p), cols(g)], p_buf.at[g],
            ps_sem.at[g, step - 1], p_sem.at[g],
            device_id={"rep": (r + step) % n_rep}, device_id_type=MESH,
        )

    def rs_copy(g, step):
        j = (me + step) % members
        return pltpu.make_async_remote_copy(
            part.at[g, j], rs_buf.at[g, step - 1],
            rs_send.at[g, step - 1], rs_recv.at[g, step - 1],
            device_id=member(j), device_id_type=MESH,
        )

    def ag_copy(g, step):
        return pltpu.make_async_remote_copy(
            ag_buf.at[g, me], ag_buf.at[g, me],
            ag_send.at[g, step - 1], ag_recv.at[g, step - 1],
            device_id=member((me + step) % members), device_id_type=MESH,
        )

    def ag_arrival(g, step):
        source = (me + members - step) % members
        return pltpu.make_async_remote_copy(
            ag_buf.at[g, source], ag_buf.at[g, source],
            ag_send.at[g, step - 1], ag_recv.at[g, step - 1],
            device_id=member((me + step) % members), device_id_type=MESH,
        )

    def col_copy(g, step):
        target = member(x * chunks + g)
        target["pts"] = (x + step) % n_pts
        return pltpu.make_async_remote_copy(
            ag_buf.at[g, me], col_buf.at[me],
            col_send.at[g, step - 1], col_recv.at[me],
            device_id=target, device_id_type=MESH,
        )

    def col_arrival(i):
        return pltpu.make_async_remote_copy(
            ag_buf.at[0, i], col_buf.at[i], col_send.at[0, 0], col_recv.at[i],
            device_id={"pts": home}, device_id_type=MESH,
        )

    q_copy(0).start()
    for i in range(n_k // group):
        d_copy(i).start()
    for g in range(1, chunks):
        q_copy(g).start()

    barrier = pltpu.get_barrier_semaphore()
    for step in range(1, members):
        pl.semaphore_signal(
            barrier, inc=1, device_id=member((me + step) % members), device_id_type=MESH
        )

    @pl.when(home != x)
    def _():
        for i in range(members):
            source = {"aux": i // n_rep, "rep": i % n_rep, "pts": home}
            pl.semaphore_signal(barrier, inc=1, device_id=source, device_id_type=MESH)

    @pl.when(owner == r)
    def _():
        for g in range(chunks):
            p_local(g).start()

    pl.semaphore_wait(barrier, members - 1 + (n_pts - 1) * chunks)

    @pl.when(owner == r)
    def _():
        for g in range(chunks):
            for step in range(1, n_rep):
                p_remote(g, step).start()

    def finish(g):
        for step in range(1, members):
            rs_copy(g, step).wait_recv()
        total = part[g, me]
        for step in range(1, members):
            total = total + rs_buf[g, step - 1]
        ag_buf[g, me] = total
        for step in range(1, members):
            ag_copy(g, step).start()
        for step in range(1, n_pts):
            col_copy(g, step).start()

    def chunk(g, carry):
        q_copy(g).wait()

        @pl.when(g == 0)
        def _():
            for i in range(n_k // group):
                d_copy(i).wait()

        @pl.when(owner == r)
        def _():
            p_local(g).wait()

        @pl.when(owner != r)
        def _():
            p_remote(g, 1).wait_recv()

        for t in range(0, width, tile):
            q_rows = q_buf[g, :, t : t + tile]
            p_rows = p_buf[g, :, t : t + tile].astype(jnp.float32)
            for k in range(0, n_k, group):
                lhs = d_buf[k : k + group].reshape(group * n_p, n_q)
                c = jnp.dot(lhs, q_rows, preferred_element_type=jnp.float32)
                for j in range(group):
                    term = c[j * n_p : (j + 1) * n_p] * p_rows
                    row = (k + j) % rows
                    part[g, (k + j) // rows, row : row + 1, t : t + tile] = jnp.sum(
                        term, axis=0, keepdims=True
                    )
        for step in range(1, members):
            rs_copy(g, step).start()

        @pl.when(g > 0)
        def _():
            finish(g - 1)

        return carry

    lax.fori_loop(0, chunks, chunk, 0)
    finish(chunks - 1)

    for g in range(chunks):
        for step in range(1, members):
            ag_arrival(g, step).wait_recv()
        for i in range(members):
            flat[i * rows : (i + 1) * rows, :] = ag_buf[g, i]
        high, low = split(flat[...])
        there = slice(g * width, (g + 1) * width)
        left_ref[0:n_k, there] = high
        left_ref[n_k : 2 * n_k, there] = high
        left_ref[2 * n_k : 3 * n_k, there] = low

    @pl.when(home == x)
    def _():
        for i in range(members):
            col_flat[i * rows : (i + 1) * rows, :] = ag_buf[me % chunks, i]

    @pl.when(home != x)
    def _():
        for i in range(members):
            col_arrival(i).wait_recv()
            col_flat[i * rows : (i + 1) * rows, :] = col_buf[i]

    high, low = split(col_flat[...])
    right_ref[0:n_k, :] = high
    right_ref[n_k : 2 * n_k, :] = low
    right_ref[2 * n_k : 3 * n_k, :] = high

    for g in range(chunks):
        for step in range(1, members):
            rs_copy(g, step).wait_send()
            ag_copy(g, step).wait_send()
        for step in range(1, n_pts):
            col_copy(g, step).wait_send()

    @pl.when(owner == r)
    def _():
        for g in range(chunks):
            for step in range(1, n_rep):
                p_remote(g, step).wait_send()


def factors(density, orbitals, group=4, tile=512):
    n_k, n_p, n_q = density.shape
    own_pts = orbitals.shape[1]
    n_aux, n_pts, n_rep = (lax.axis_size(name) for name in ("aux", "pts", "rep"))
    members = n_aux * n_rep
    chunks = members // n_pts
    width = own_pts // chunks
    rows = n_k // members
    dma = pltpu.SemaphoreType.DMA
    f32, bf16 = jnp.float32, jnp.bfloat16
    return pl.pallas_call(
        functools.partial(share_kernel, (n_aux, n_pts, n_rep, group, min(tile, width))),
        in_specs=[pl.BlockSpec(memory_space=pl.ANY)] * 2,
        out_specs=[pl.BlockSpec(memory_space=pltpu.VMEM)] * 2,
        out_shape=[
            jax.ShapeDtypeStruct((3 * n_k, own_pts), bf16),
            jax.ShapeDtypeStruct((3 * n_k, width), bf16),
        ],
        scratch_shapes=[
            pltpu.VMEM((n_k, n_p, n_q), bf16),
            pltpu.VMEM((chunks, n_q, width), bf16),
            pltpu.VMEM((chunks, n_p, width), bf16),
            pltpu.VMEM((chunks, members, rows, width), f32),
            pltpu.VMEM((chunks, members - 1, rows, width), f32),
            pltpu.VMEM((chunks, members, rows, width), f32),
            pltpu.VMEM((members, rows, width), f32),
            pltpu.VMEM((n_k, width), f32),
            pltpu.VMEM((n_k, width), f32),
            dma((n_k // group,)),
            dma((chunks,)),
            dma((chunks,)),
            dma((chunks, n_rep - 1)),
            dma((chunks, members - 1)),
            dma((chunks, members - 1)),
            dma((chunks, members - 1)),
            dma((chunks, members - 1)),
            dma((chunks, n_pts - 1)),
            dma((members,)),
        ],
        compiler_params=pltpu.CompilerParams(
            collective_id=0, has_side_effects=True, vmem_limit_bytes=48 << 20
        ),
        cost_estimate=pl.CostEstimate(
            flops=2 * n_k * n_p * n_q * own_pts,
            bytes_accessed=2 * (n_k * n_p * n_q + (n_p + n_q) * own_pts),
            transcendentals=0,
        ),
    )(density, orbitals)


def outer_kernel(scale, left_ref, right_ref, o_ref):
    o_ref[...] = (
        lax.dot_general(
            left_ref[...], right_ref[...], (((0,), (0,)), ((), ())),
            preferred_element_type=jnp.float32,
        )
        * scale
    )


def outer(left, right, scale, tile=512):
    depth, n_rows = left.shape
    n_cols = right.shape[1]
    tile = min(tile, n_rows)
    return pl.pallas_call(
        functools.partial(outer_kernel, scale),
        grid=(n_rows // tile,),
        in_specs=[
            pl.BlockSpec((depth, tile), lambda i: (0, i)),
            pl.BlockSpec((depth, n_cols), lambda i: (0, 0)),
        ],
        out_specs=pl.BlockSpec((tile, n_cols), lambda i: (i, 0)),
        out_shape=jax.ShapeDtypeStruct((n_rows, n_cols), jnp.float32),
        compiler_params=pltpu.CompilerParams(vmem_limit_bytes=32 << 20),
    )(left, right)


def per_device(density_slab, orbitals):
    left, right = factors(density_slab, orbitals)
    return outer(left, right, 1.0 / density_slab.shape[0])


def solution(mesh):
    return jax.shard_map(
        per_device,
        mesh=mesh,
        in_specs=(P("groups", "aux", "rep"), P(("groups", "rep"), "pts")),
        out_specs=P(("groups", "pts"), ("aux", "rep")),
        check_vma=False,
    )
```

time: 206 us -> 44.3 us (0.22)
  blocking collectives: 121 us -> 0 us
  Pallas kernels: 0 us -> 41.9 us
  matrix products: 38.3 us -> 0 us
  waiting for transfers between devices: 18 us -> 0 us
  between operations: 13.4 us -> 0.01 us
  other arithmetic: 12 us -> 0 us
    all_to_all x1 -> x0, blocking collectives: 99.5 us -> none  [per_device(): lax.all_to_all(density_slab, 'aux', split_axis=0, concat_axis=1, tiled=True)]
    pallas_call x0 -> x2, Pallas kernels: none -> 41.9 us  [the longest x1 34.1 us: factors(): pl.pallas_call(functools.partial(share_kernel, (n_aux, n_pts, n_rep, grou...]
    dot_general x2 -> x0, matrix products: 38.3 us -> none  [the longest x1 22.4 us: per_device(): jnp.einsum('kpq,qs->kps', regrouped, orbitals, preferred_element_type=jnp...]
    all_gather x2 -> x0, blocking collectives: 21.7 us -> none  [the longest x1 14.4 us: per_device(): own_w = lax.all_gather(summed, 'aux', axis=0, tiled=True)]
    psum x1 -> x0, waiting for transfers between devices: 17.2 us -> none  [per_device(): summed = lax.psum(partial_w, 'rep')]
    convert_element_type x1 -> x0, other arithmetic: 12 us -> none  [per_device(): partial_w = jnp.sum(full_orbitals[None] * contracted, axis=1)]
    all_to_all x1 -> x0, local copies, waits for them, and re-layouts: 2.38 us -> none  [per_device(): lax.all_to_all(density_slab, 'aux', split_axis=0, concat_axis=1, tiled=True)]
    unnamed x3 -> x2, local copies, waits for them, and re-layouts: 0.09 us -> 2.19 us
  transfers between devices with their start and end apart: 2 -> 0, of which waited for: 1 -> 0; matrix products, arithmetic and copies ran while one was open for 1% -> 0% of each run, Pallas kernels for 0% -> 0%
where the time goes in v2:
time: 44.3 us; the launch traced here: 44.1 us
  Pallas kernels  41.9 us (95%)
  local copies, waits for them, and re-layouts  2.19 us (5%)
    pallas_call x1, Pallas kernels, factors(): pl.pallas_call(functools.partial(share_kernel, (n_aux, n_pts, n_rep, grou...  34.1 us
    pallas_call x1, Pallas kernels, outer(): pl.pallas_call(functools.partial(outer_kernel, scale), grid=(n_rows // ti...  7.84 us
    unnamed x2, local copies, waits for them, and re-layouts  2.19 us

profile of v2, /device:TPU:0, one launch (start us, length us, event | category | flops | bytes accessed | tf_op | source)
XLA Modules:
  0.0 44.1 jit_solution(5038635646617940440)
XLA Ops:
  0.0 0.0 copy-start
  0.0 2.2 %copy-done = bf16[16,256,512]{2,1,0:T(8,128)(2,1)S(1)} copy-done((bf16[16,256,512]{2,1,0:T(8,128)(2,1)S(1)}, bf16[16,256,512]{2,1,0:T(8,128)(2,1)}, u32[]{:S(2)}) %copy-start) | copy-done | bytes 4194328
  2.2 34.1 %shard_map.28 = (bf16[48,4096]{1,0:T(8,128)(2,1)S(1)}, bf16[48,1024]{1,0:T(8,128)(2,1)S(1)}) custom-call(bf16[16,256,512]{2,1,0:T(8,128)(2,1)S(1)} %copy-done, bf16[512,4096]{1,0:T(8,128)(2,1)} %orb_hbm.1), custom_call_target="tpu_custom_call" | custom-call | flops 17179869184 | bytes 10485760 | tf_op jit(solution)/shard_map/pallas_call | solution.py:231
  36.3 7.8 %shard_map.29 = f32[4096,1024]{1,0:T(8,128)} custom-call(bf16[48,4096]{1,0:T(8,128)(2,1)S(1)} %get-tuple-element.7.left_ref, bf16[48,1024]{1,0:T(8,128)(2,1)S(1)} %get-tuple-element.8.right_ref), custom_call_target="tpu_custom_call" | custom-call | tf_op jit(solution)/shard_map/pallas_call | solution.py:285
Async XLA Ops:
  0.0 2.2 %copy-start = (bf16[16,256,512]{2,1,0:T(8,128)(2,1)S(1)}, bf16[16,256,512]{2,1,0:T(8,128)(2,1)}, u32[]{:S(2)}) copy-start(bf16[16,256,512]{2,1,0:T(8,128)(2,1)} %d_hbm.1) | copy-start | bytes 12582916

commit v3 on v2

--- a/solution.py
+++ b/solution.py
@@ -258,7 +258,7 @@
             dma((members,)),
         ],
         compiler_params=pltpu.CompilerParams(
-            collective_id=0, has_side_effects=True, vmem_limit_bytes=48 << 20
+            collective_id=0, has_side_effects=True, vmem_limit_bytes=60 << 20
         ),
         cost_estimate=pl.CostEstimate(
             flops=2 * n_k * n_p * n_q * own_pts,
@@ -268,30 +268,60 @@
     )(density, orbitals)
 
 
-def outer_kernel(scale, left_ref, right_ref, o_ref):
-    o_ref[...] = (
-        lax.dot_general(
-            left_ref[...], right_ref[...], (((0,), (0,)), ((), ())),
-            preferred_element_type=jnp.float32,
-        )
-        * scale
-    )
-
-
-def outer(left, right, scale, tile=512):
-    depth, n_rows = left.shape
-    n_cols = right.shape[1]
-    tile = min(tile, n_rows)
+def outer_kernel(
+    scale, tile, slots, left_hbm, right_hbm, o_ref, left, right, buf, in_sem, sem
+):
+    steps = o_ref.shape[0] // tile
+    parts = in_sem.shape[0] - 1
+    width = o_ref.shape[0] // parts
+
+    def fetch(g):
+        there = pl.ds(g * width, width)
+        return pltpu.make_async_copy(left_hbm.at[:, there], left.at[:, there], in_sem.at[g])
+
+    def store(i):
+        return pltpu.make_async_copy(
+            buf.at[i % slots], o_ref.at[pl.ds(i * tile, tile)], sem.at[i % slots]
+        )
+
+    whole = pltpu.make_async_copy(right_hbm, right, in_sem.at[parts])
+    whole.start()
+    for g in range(parts):
+        fetch(g).start()
+    whole.wait()
+    for i in range(steps):
+        if i * tile % width == 0:
+            fetch(i * tile // width).wait()
+        if i >= slots:
+            store(i - slots).wait()
+        buf[i % slots] = (
+            lax.dot_general(
+                left[:, i * tile : (i + 1) * tile], right[...],
+                (((0,), (0,)), ((), ())), preferred_element_type=jnp.float32,
+            )
+            * scale
+        )
+        store(i).start()
+    for i in range(max(0, steps - slots), steps):
+        store(i).wait()
+
+
+def outer(left, right, scale, tile=256, slots=4, parts=4):
+    n_rows, n_cols = left.shape[1], right.shape[1]
+    tile = min(tile, n_rows // parts)
     return pl.pallas_call(
-        functools.partial(outer_kernel, scale),
-        grid=(n_rows // tile,),
-        in_specs=[
-            pl.BlockSpec((depth, tile), lambda i: (0, i)),
-            pl.BlockSpec((depth, n_cols), lambda i: (0, 0)),
+        functools.partial(outer_kernel, scale, tile, slots),
+        in_specs=[pl.BlockSpec(memory_space=pl.ANY)] * 2,
+        out_specs=pl.BlockSpec(memory_space=pl.ANY),
+        out_shape=jax.ShapeDtypeStruct((n_rows, n_cols), jnp.float32),
+        scratch_shapes=[
+            pltpu.VMEM(left.shape, left.dtype),
+            pltpu.VMEM(right.shape, right.dtype),
+            pltpu.VMEM((slots, tile, n_cols), jnp.float32),
+            pltpu.SemaphoreType.DMA((parts + 1,)),
+            pltpu.SemaphoreType.DMA((slots,)),
         ],
-        out_specs=pl.BlockSpec((tile, n_cols), lambda i: (i, 0)),
-        out_shape=jax.ShapeDtypeStruct((n_rows, n_cols), jnp.float32),
-        compiler_params=pltpu.CompilerParams(vmem_limit_bytes=32 << 20),
+        compiler_params=pltpu.CompilerParams(vmem_limit_bytes=62 << 20),
     )(left, right)
 
 

time: 44.3 us -> 42.1 us (0.950)
  local copies, waits for them, and re-layouts: 2.19 us -> 0 us
    unnamed x2 -> x0, local copies, waits for them, and re-layouts: 2.19 us -> none
    pallas_call x1, Pallas kernels: 34.1 us -> 34.8 us  [factors(): pl.pallas_call(functools.partial(share_kernel, (n_aux, n_pts, n_rep, grou...]
    pallas_call x1, Pallas kernels: 7.84 us -> 7.22 us  [outer(): pl.pallas_call(functools.partial(outer_kernel, scale, tile, slots), in_sp...]
where the time goes in v3:
time: 42.1 us; the launch traced here: 42 us
  Pallas kernels  42 us (100%)
    pallas_call x1, Pallas kernels, factors(): pl.pallas_call(functools.partial(share_kernel, (n_aux, n_pts, n_rep, grou...  34.8 us
    pallas_call x1, Pallas kernels, outer(): pl.pallas_call(functools.partial(outer_kernel, scale, tile, slots), in_sp...  7.22 us

profile of v3, /device:TPU:0, one launch (start us, length us, event | category | flops | bytes accessed | tf_op | source)
XLA Modules:
  0.0 42.0 jit_solution(17445096871040216890)
XLA Ops:
  0.0 34.8 %shard_map.28 = (bf16[48,4096]{1,0:T(8,128)(2,1)}, bf16[48,1024]{1,0:T(8,128)(2,1)}) custom-call(bf16[16,256,512]{2,1,0:T(8,128)(2,1)} %d_hbm.1, bf16[512,4096]{1,0:T(8,128)(2,1)} %orb_hbm.1), custom_call_target="tpu_custom_call" | custom-call | flops 17179869184 | bytes 10485760 | tf_op jit(solution)/shard_map/pallas_call | solution.py:231
  34.8 7.2 %shard_map.29 = f32[4096,1024]{1,0:T(8,128)} custom-call(bf16[48,4096]{1,0:T(8,128)(2,1)} %get-tuple-element.7.left_hbm, bf16[48,1024]{1,0:T(8,128)(2,1)} %get-tuple-element.8.right_hbm), custom_call_target="tpu_custom_call" | custom-call | tf_op jit(solution)/shard_map/pallas_call | solution.py:312

commit v4 on v3

--- a/solution.py
+++ b/solution.py
@@ -94,8 +94,9 @@
             device_id={"pts": home}, device_id_type=MESH,
         )
 
+    d_copy(0).start()
     q_copy(0).start()
-    for i in range(n_k // group):
+    for i in range(1, n_k // group):
         d_copy(i).start()
     for g in range(1, chunks):
         q_copy(g).start()
@@ -137,13 +138,8 @@
         for step in range(1, n_pts):
             col_copy(g, step).start()
 
-    def chunk(g, carry):
+    def chunk(g, opening):
         q_copy(g).wait()
-
-        @pl.when(g == 0)
-        def _():
-            for i in range(n_k // group):
-                d_copy(i).wait()
 
         @pl.when(owner == r)
         def _():
@@ -157,6 +153,8 @@
             q_rows = q_buf[g, :, t : t + tile]
             p_rows = p_buf[g, :, t : t + tile].astype(jnp.float32)
             for k in range(0, n_k, group):
+                if opening and t == 0:
+                    d_copy(k // group).wait()
                 lhs = d_buf[k : k + group].reshape(group * n_p, n_q)
                 c = jnp.dot(lhs, q_rows, preferred_element_type=jnp.float32)
                 for j in range(group):
@@ -165,19 +163,12 @@
                     part[g, (k + j) // rows, row : row + 1, t : t + tile] = jnp.sum(
                         term, axis=0, keepdims=True
                     )
+            if t == 0 and not opening:
+                finish(g - 1)
         for step in range(1, members):
             rs_copy(g, step).start()
 
-        @pl.when(g > 0)
-        def _():
-            finish(g - 1)
-
-        return carry
-
-    lax.fori_loop(0, chunks, chunk, 0)
-    finish(chunks - 1)
-
-    for g in range(chunks):
+    def assemble(g):
         for step in range(1, members):
             ag_arrival(g, step).wait_recv()
         for i in range(members):
@@ -188,6 +179,33 @@
         left_ref[n_k : 2 * n_k, there] = high
         left_ref[2 * n_k : 3 * n_k, there] = low
 
+    def drain(g):
+        for step in range(1, members):
+            rs_copy(g, step).wait_send()
+            ag_copy(g, step).wait_send()
+        for step in range(1, n_pts):
+            col_copy(g, step).wait_send()
+
+    chunk(0, True)
+
+    def later(g, carry):
+        chunk(g, False)
+        return carry
+
+    lax.fori_loop(1, chunks, later, 0)
+    for g in range(chunks - 1):
+        assemble(g)
+        drain(g)
+
+    @pl.when(owner == r)
+    def _():
+        for g in range(chunks):
+            for step in range(1, n_rep):
+                p_remote(g, step).wait_send()
+
+    finish(chunks - 1)
+    assemble(chunks - 1)
+
     @pl.when(home == x)
     def _():
         for i in range(members):
@@ -203,19 +221,7 @@
     right_ref[0:n_k, :] = high
     right_ref[n_k : 2 * n_k, :] = low
     right_ref[2 * n_k : 3 * n_k, :] = high
-
-    for g in range(chunks):
-        for step in range(1, members):
-            rs_copy(g, step).wait_send()
-            ag_copy(g, step).wait_send()
-        for step in range(1, n_pts):
-            col_copy(g, step).wait_send()
-
-    @pl.when(owner == r)
-    def _():
-        for g in range(chunks):
-            for step in range(1, n_rep):
-                p_remote(g, step).wait_send()
+    drain(chunks - 1)
 
 
 def factors(density, orbitals, group=4, tile=512):

time: 42.1 us -> 46.6 us (1.11)
  Pallas kernels: 42 us -> 46.5 us
    pallas_call x1, Pallas kernels: 34.8 us -> 39.2 us  [factors(): pl.pallas_call(functools.partial(share_kernel, (n_aux, n_pts, n_rep, grou...]
where the time goes in v4:
time: 46.6 us; the launch traced here: 46.5 us
  Pallas kernels  46.5 us (100%)
    pallas_call x1, Pallas kernels, factors(): pl.pallas_call(functools.partial(share_kernel, (n_aux, n_pts, n_rep, grou...  39.2 us
    pallas_call x1, Pallas kernels, outer(): pl.pallas_call(functools.partial(outer_kernel, scale, tile, slots), in_sp...  7.22 us

profile of v4, /device:TPU:0, one launch (start us, length us, event | category | flops | bytes accessed | tf_op | source)
XLA Modules:
  0.0 46.5 jit_solution(7946786253129629914)
XLA Ops:
  0.0 39.2 %shard_map.28 = (bf16[48,4096]{1,0:T(8,128)(2,1)}, bf16[48,1024]{1,0:T(8,128)(2,1)}) custom-call(bf16[16,256,512]{2,1,0:T(8,128)(2,1)} %d_hbm.1, bf16[512,4096]{1,0:T(8,128)(2,1)} %orb_hbm.1), custom_call_target="tpu_custom_call" | custom-call | flops 17179869184 | bytes 10485760 | tf_op jit(solution)/shard_map/pallas_call | solution.py:237
  39.3 7.2 %shard_map.29 = f32[4096,1024]{1,0:T(8,128)} custom-call(bf16[48,4096]{1,0:T(8,128)(2,1)} %get-tuple-element.7.left_hbm, bf16[48,1024]{1,0:T(8,128)(2,1)} %get-tuple-element.8.right_hbm), custom_call_target="tpu_custom_call" | custom-call | tf_op jit(solution)/shard_map/pallas_call | solution.py:318

commit v5 on v4

--- a/solution.py
+++ b/solution.py
@@ -138,8 +138,13 @@
         for step in range(1, n_pts):
             col_copy(g, step).start()
 
-    def chunk(g, opening):
+    def chunk(g, carry):
         q_copy(g).wait()
+
+        @pl.when(g == 0)
+        def _():
+            for i in range(n_k // group):
+                d_copy(i).wait()
 
         @pl.when(owner == r)
         def _():
@@ -153,8 +158,6 @@
             q_rows = q_buf[g, :, t : t + tile]
             p_rows = p_buf[g, :, t : t + tile].astype(jnp.float32)
             for k in range(0, n_k, group):
-                if opening and t == 0:
-                    d_copy(k // group).wait()
                 lhs = d_buf[k : k + group].reshape(group * n_p, n_q)
                 c = jnp.dot(lhs, q_rows, preferred_element_type=jnp.float32)
                 for j in range(group):
@@ -163,10 +166,14 @@
                     part[g, (k + j) // rows, row : row + 1, t : t + tile] = jnp.sum(
                         term, axis=0, keepdims=True
                     )
-            if t == 0 and not opening:
-                finish(g - 1)
         for step in range(1, members):
             rs_copy(g, step).start()
+
+        @pl.when(g > 0)
+        def _():
+            finish(g - 1)
+
+        return carry
 
     def assemble(g):
         for step in range(1, members):
@@ -186,13 +193,7 @@
         for step in range(1, n_pts):
             col_copy(g, step).wait_send()
 
-    chunk(0, True)
-
-    def later(g, carry):
-        chunk(g, False)
-        return carry
-
-    lax.fori_loop(1, chunks, later, 0)
+    lax.fori_loop(0, chunks, chunk, 0)
     for g in range(chunks - 1):
         assemble(g)
         drain(g)

time: 46.6 us -> 42.8 us (0.918)
  Pallas kernels: 46.5 us -> 42.7 us
    pallas_call x1, Pallas kernels: 39.2 us -> 35.5 us  [factors(): pl.pallas_call(functools.partial(share_kernel, (n_aux, n_pts, n_rep, grou...]
where the time goes in v5:
time: 42.8 us; the launch traced here: 42.7 us
  Pallas kernels  42.7 us (100%)
    pallas_call x1, Pallas kernels, factors(): pl.pallas_call(functools.partial(share_kernel, (n_aux, n_pts, n_rep, grou...  35.5 us
    pallas_call x1, Pallas kernels, outer(): pl.pallas_call(functools.partial(outer_kernel, scale, tile, slots), in_sp...  7.21 us

profile of v5, /device:TPU:0, one launch (start us, length us, event | category | flops | bytes accessed | tf_op | source)
XLA Modules:
  0.0 42.7 jit_solution(13388096312538156925)
XLA Ops:
  0.0 35.5 %shard_map.28 = (bf16[48,4096]{1,0:T(8,128)(2,1)}, bf16[48,1024]{1,0:T(8,128)(2,1)}) custom-call(bf16[16,256,512]{2,1,0:T(8,128)(2,1)} %d_hbm.1, bf16[512,4096]{1,0:T(8,128)(2,1)} %orb_hbm.1), custom_call_target="tpu_custom_call" | custom-call | flops 17179869184 | bytes 10485760 | tf_op jit(solution)/shard_map/pallas_call | solution.py:238
  35.5 7.2 %shard_map.29 = f32[4096,1024]{1,0:T(8,128)} custom-call(bf16[48,4096]{1,0:T(8,128)(2,1)} %get-tuple-element.7.left_hbm, bf16[48,1024]{1,0:T(8,128)(2,1)} %get-tuple-element.8.right_hbm), custom_call_target="tpu_custom_call" | custom-call | tf_op jit(solution)/shard_map/pallas_call | solution.py:319

commit v6 on v5

--- a/solution.py
+++ b/solution.py
@@ -194,7 +194,7 @@
             col_copy(g, step).wait_send()
 
     lax.fori_loop(0, chunks, chunk, 0)
-    for g in range(chunks - 1):
+    for g in range(chunks - 2):
         assemble(g)
         drain(g)
 
@@ -205,7 +205,8 @@
                 p_remote(g, step).wait_send()
 
     finish(chunks - 1)
-    assemble(chunks - 1)
+    for g in range(chunks - 2, chunks):
+        assemble(g)
 
     @pl.when(home == x)
     def _():
@@ -222,10 +223,11 @@
     right_ref[0:n_k, :] = high
     right_ref[n_k : 2 * n_k, :] = low
     right_ref[2 * n_k : 3 * n_k, :] = high
-    drain(chunks - 1)
-
-
-def factors(density, orbitals, group=4, tile=512):
+    for g in range(chunks - 2, chunks):
+        drain(g)
+
+
+def factors(density, orbitals, group=2, tile=1024):
     n_k, n_p, n_q = density.shape
     own_pts = orbitals.shape[1]
     n_aux, n_pts, n_rep = (lax.axis_size(name) for name in ("aux", "pts", "rep"))

time: 42.8 us -> 42 us (0.981)
  Pallas kernels: 42.7 us -> 41.9 us
    pallas_call x1, Pallas kernels: 35.5 us -> 34.7 us  [factors(): pl.pallas_call(functools.partial(share_kernel, (n_aux, n_pts, n_rep, grou...]
where the time goes in v6:
time: 42 us; the launch traced here: 41.9 us
  Pallas kernels  41.9 us (100%)
    pallas_call x1, Pallas kernels, factors(): pl.pallas_call(functools.partial(share_kernel, (n_aux, n_pts, n_rep, grou...  34.7 us
    pallas_call x1, Pallas kernels, outer(): pl.pallas_call(functools.partial(outer_kernel, scale, tile, slots), in_sp...  7.21 us

profile of v6, /device:TPU:0, one launch (start us, length us, event | category | flops | bytes accessed | tf_op | source)
XLA Modules:
  0.0 41.9 jit_solution(13391844248453859779)
XLA Ops:
  0.0 34.7 %shard_map.28 = (bf16[48,4096]{1,0:T(8,128)(2,1)}, bf16[48,1024]{1,0:T(8,128)(2,1)}) custom-call(bf16[16,256,512]{2,1,0:T(8,128)(2,1)} %d_hbm.1, bf16[512,4096]{1,0:T(8,128)(2,1)} %orb_hbm.1), custom_call_target="tpu_custom_call" | custom-call | flops 17179869184 | bytes 10485760 | tf_op jit(solution)/shard_map/pallas_call | solution.py:240
  34.7 7.2 %shard_map.29 = f32[4096,1024]{1,0:T(8,128)} custom-call(bf16[48,4096]{1,0:T(8,128)(2,1)} %get-tuple-element.7.left_hbm, bf16[48,1024]{1,0:T(8,128)(2,1)} %get-tuple-element.8.right_hbm), custom_call_target="tpu_custom_call" | custom-call | tf_op jit(solution)/shard_map/pallas_call | solution.py:321
